TPU v7x, 128 devices: a whole 4x4x4 slice. The times are simulated.
128 devices in a mesh: dp: 32 (over x, z, core), enc: 4 (over y).
Axes of the slice: x: 4, y: 4, z: 4, core: 2. Of those that a mesh axis runs over, the one named last changes fastest.
Arguments:
- hidden: bfloat16 [16384, 4096], P('dp', 'enc'), may hold values from -6 to 6
- norm_gain: float32 [4096], replicated, may hold values from 0.25 to 1.75
- w_query: bfloat16 [4096, 2048], P('dp', 'enc'), may hold values from -0.09375 to 0.09375
- w_key: bfloat16 [896, 2048], P('dp', 'enc'), may hold values from -0.1875 to 0.1875
- w_value: bfloat16 [896, 2048], P('dp', 'enc'), may hold values from -0.1875 to 0.1875
- w_out: bfloat16 [2048, 4096], P('enc', 'dp'), may hold values from -0.125 to 0.125
- w_cond: bfloat16 [4096, 896], P('dp', 'enc'), may hold values from -0.75 to 0.75
- enc_gain: float32 [896], replicated, may hold values from 0.25 to 1.75
- store: bfloat16 [1024, 128, 896], P(('dp', 'enc')), may hold values from -6 to 6
- neighbour_ids: int32 [512], P(('dp', 'enc')), may hold values from 0 to 1023, as said below
- out_grad: bfloat16 [16384, 4096], P('dp', 'enc'), may hold values from -6 to 6
Outputs:
- layer_out: bfloat16 [16384, 4096], P('dp', 'enc')
- hidden_grad: float32 [16384, 4096], P('dp', 'enc')
- query_grad: float32 [4096, 2048], P('dp', 'enc')
- key_grad: float32 [896, 2048], P('dp', 'enc')
- value_grad: float32 [896, 2048], P('dp', 'enc')
- out_weight_grad: float32 [2048, 4096], P('enc', 'dp')
- cond_grad: float32 [4096, 896], P('dp', 'enc')
Inputs may be any that keep to these rules, and one draw needn't show every extreme that they name: `neighbour_ids`: slot n names a neighbour stored on a device of the same data index as the device holding slot n (device k holds rows k * 8 to (k + 1) * 8 - 1). Among the 4 slots of one device at most 2 name rows of one device, and for every data index one device is named by exactly 2 slots of each of the 4 devices.
All inputs are finite; a program needn't handle non-finite values.
Results may differ from a plain program's by a relative error of at most 0.019.
Values may be sent and summed in bfloat16 or wider, within the bound.
A program may use at most 192 MiB of HBM per device.

v0:
```python
import jax
import jax.numpy as jnp
from jax import lax
from jax.sharding import PartitionSpec as P

HSZ = 128
SPAN = 64
NBR = 2
NL = 128
epsilon = 1e-05


def side_by_side(arrays, axis, dim, along):
    ends, at = ([], 0)
    for a in arrays[:-1]:
        at += a.shape[along]
        ends.append(at)
    both = jnp.concatenate(arrays, axis=along)
    return tuple(jnp.split(lax.all_gather(both, axis, axis=dim, tiled=True), ends, axis=along))


def joined_along(tiles, dim):
    tiles = jnp.moveaxis(tiles, 0, dim)
    dims = tiles.shape
    return tiles.reshape(*dims[:dim], dims[dim] * dims[dim + 1], *dims[dim + 2 :])


def copy_for_each(shard, axis):
    copies = jnp.broadcast_to(shard, (lax.axis_size(axis), *shard.shape))
    return lax.all_to_all(copies, axis, split_axis=0, concat_axis=0, tiled=True)


def collect(shard, axis, dim):
    return joined_along(copy_for_each(shard, axis), dim)


def in_blocks(shard, dim, peers):
    dims = shard.shape
    tiles = shard.reshape(*dims[:dim], peers, dims[dim] // peers, *dims[dim + 1 :])
    return jnp.moveaxis(tiles, dim, 0)


def summed_on_arrival(shard, axis, dim):
    peers = lax.axis_size(axis)
    tiles = lax.all_to_all(in_blocks(shard, dim, peers), axis, 0, 0, tiled=True)
    return jnp.sum(tiles.astype(jnp.float32), axis=0)


def one_scatter(arrays, axis, dims):
    peers = lax.axis_size(axis)
    tiles = [in_blocks(a, dim, peers) for a, dim in zip(arrays, dims)]
    lines = jnp.concatenate([b.reshape(peers, -1) for b in tiles], axis=1)
    extent = max(16, -(-lines.shape[1] // 1024) * 8)
    lines = jnp.pad(lines, ((0, 0), (0, extent * 128 - lines.shape[1]))).reshape(-1, 128)
    flat, at, done = (lax.psum_scatter(lines, axis, tiled=True).reshape(-1), 0, [])
    for b in tiles:
        part = b[0]
        done.append(flat[at : at + part.size].reshape(part.shape))
        at += part.size
    return tuple(done)


def rms_scale(values):
    return lax.rsqrt(jnp.mean(values * values, axis=-1, keepdims=True) + epsilon)


def encoder_input(raw_rows, cond_rows):
    enc_in = raw_rows.astype(jnp.float32) + cond_rows.astype(jnp.float32)[..., None, :]
    return (enc_in, rms_scale(enc_in))


def encode_rows(raw_rows, cond_rows, enc_gain):
    enc_in, enc_rstd = encoder_input(raw_rows, cond_rows)
    return (enc_in * enc_rstd * enc_gain).astype(jnp.bfloat16)


def cond_gradient(raw_rows, cond_rows, enc_gain, grad_rows):
    enc_in, enc_rstd = encoder_input(raw_rows, cond_rows)
    scaled_enc = enc_gain * grad_rows.astype(jnp.float32)
    enc_mean = jnp.mean(enc_in * scaled_enc, axis=-1, keepdims=True)
    return jnp.sum(enc_rstd * scaled_enc - enc_in * enc_rstd**3 * enc_mean, axis=-2)


def contract_first(left, right):
    return lax.dot_general(
        left, right, (((0,), (0,)), ((), ())), preferred_element_type=jnp.float32
    )


def contract_last(left, right):
    return lax.dot_general(
        left, right, (((1,), (1,)), ((), ())), preferred_element_type=jnp.float32
    )


def shards(
    hidden,
    norm_gain,
    w_query,
    w_key,
    w_value,
    w_out,
    w_cond,
    enc_gain,
    store,
    neighbour_ids,
    out_grad,
):
    groups = lax.axis_size("enc")
    member = lax.axis_index("enc")
    tok_rows = hidden.shape[0]
    feature_cols = hidden.shape[1]
    model_width = feature_cols * groups
    head_cols = w_query.shape[1]
    enc_width = w_key.shape[0] * lax.axis_size("dp")
    enc_cols = w_cond.shape[1]
    span_count = tok_rows // SPAN
    requests = neighbour_ids.shape[0]
    capacity = max(2, (requests + 1) // 2)
    store_rows = store.shape[0]
    heads_here = head_cols // HSZ
    keys_len = NBR * NL
    score_scale = HSZ ** (-0.5)
    full_rows = lax.all_gather(hidden, "enc", axis=1, tiled=True)
    inputs = full_rows.astype(jnp.float32)
    row_rstd = rms_scale(inputs)
    normed = (inputs * row_rstd * norm_gain).astype(jnp.bfloat16)
    w_query_all, w_key_all, w_value_all, w_cond_all = (
        lax.all_gather(w_query, "dp", axis=0, tiled=True),
        *side_by_side((w_key, w_value), "dp", 0, 1),
        lax.all_gather(w_cond, "dp", axis=0, tiled=True),
    )
    queries = jnp.dot(normed, w_query_all, preferred_element_type=jnp.float32).astype(jnp.bfloat16)
    w_out_all = lax.all_gather(w_out, "dp", axis=1, tiled=True)
    summary = jnp.mean(inputs.reshape(span_count, SPAN, model_width), axis=1).astype(jnp.bfloat16)
    cond_part = jnp.dot(summary, w_cond_all, preferred_element_type=jnp.float32).astype(
        jnp.bfloat16
    )
    condition = collect(cond_part, "enc", 1)
    request_order = jnp.arange(requests)
    my_spans = (member * requests + request_order) // NBR
    cond_req = jnp.take(condition, my_spans, axis=0)
    owner_of = neighbour_ids // store_rows % groups
    store_row = neighbour_ids % store_rows
    earlier = (owner_of[:, None] == owner_of[None, :]) & (
        request_order[None, :] < request_order[:, None]
    )
    slot_rank = jnp.sum(earlier.astype(jnp.int32), axis=1)
    slot_index = owner_of * capacity + slot_rank
    selection = slot_index[None, :] == jnp.arange(groups * capacity)[:, None]
    row_buffer = jnp.sum(jnp.where(selection, store_row[None, :], 0), axis=1).reshape(
        groups, capacity
    )
    raw_buffer = lax.all_to_all(
        jnp.take(
            store,
            lax.all_to_all(row_buffer, "enc", split_axis=0, concat_axis=0, tiled=True),
            axis=0,
        ),
        "enc",
        split_axis=0,
        concat_axis=0,
        tiled=True,
    )
    raw_mine = jnp.take(raw_buffer.reshape(groups * capacity, NL, enc_width), slot_index, axis=0)
    encoded_mine = encode_rows(raw_mine, cond_req, enc_gain)
    encoded = lax.all_gather(encoded_mine, "enc", axis=0, tiled=True)
    flat_enc = encoded.reshape(-1, enc_width)
    keys_proj = jnp.dot(flat_enc, w_key_all, preferred_element_type=jnp.float32).astype(
        jnp.bfloat16
    )
    values_proj = jnp.dot(flat_enc, w_value_all, preferred_element_type=jnp.float32).astype(
        jnp.bfloat16
    )
    query_heads = queries.reshape(span_count, SPAN, heads_here, HSZ)
    key_heads = keys_proj.reshape(span_count, keys_len, heads_here, HSZ)
    value_heads = values_proj.reshape(span_count, keys_len, heads_here, HSZ)
    scores = (
        jnp.einsum("cqhd,ckhd->chqk", query_heads, key_heads, preferred_element_type=jnp.float32)
        * score_scale
    )
    attn_full = jax.nn.softmax(scores, axis=-1)
    attn_weights = attn_full.astype(jnp.bfloat16)
    attended = (
        jnp.einsum("chqk,ckhd->cqhd", attn_weights, value_heads, preferred_element_type=jnp.float32)
        .astype(jnp.bfloat16)
        .reshape(tok_rows, head_cols)
    )
    out_term = jnp.dot(attended, w_out_all, preferred_element_type=jnp.float32)
    projected = summed_on_arrival(out_term.astype(jnp.bfloat16), "enc", 1)
    layer_out = (hidden.astype(jnp.float32) + projected).astype(jnp.bfloat16)
    grad_rows = lax.all_gather(out_grad, "enc", axis=1, tiled=True)
    attended_grad = contract_last(grad_rows, w_out_all).astype(jnp.bfloat16)
    out_weight_grad = lax.psum_scatter(
        contract_first(attended, grad_rows).astype(jnp.bfloat16),
        "dp",
        scatter_dimension=1,
        tiled=True,
    ).astype(jnp.float32)
    grad_heads = attended_grad.reshape(span_count, SPAN, heads_here, HSZ)
    prob_grad = jnp.einsum(
        "cqhd,ckhd->chqk", grad_heads, value_heads, preferred_element_type=jnp.float32
    )
    score_grad = (
        attn_full
        * (prob_grad - jnp.sum(attn_full * prob_grad, axis=-1, keepdims=True))
        * score_scale
    ).astype(jnp.bfloat16)
    query_act_grad = (
        jnp.einsum("chqk,ckhd->cqhd", score_grad, key_heads, preferred_element_type=jnp.float32)
        .astype(jnp.bfloat16)
        .reshape(tok_rows, head_cols)
    )
    key_act_grad = (
        jnp.einsum("chqk,cqhd->ckhd", score_grad, query_heads, preferred_element_type=jnp.float32)
        .astype(jnp.bfloat16)
        .reshape(-1, head_cols)
    )
    value_act_grad = (
        jnp.einsum("chqk,cqhd->ckhd", attn_weights, grad_heads, preferred_element_type=jnp.float32)
        .astype(jnp.bfloat16)
        .reshape(-1, head_cols)
    )
    query_grad = lax.psum_scatter(
        contract_first(normed, query_act_grad).astype(jnp.bfloat16),
        "dp",
        scatter_dimension=0,
        tiled=True,
    ).astype(jnp.float32)
    enc_term = contract_last(key_act_grad, w_key_all) + contract_last(value_act_grad, w_value_all)
    encoded_grad = (
        summed_on_arrival(enc_term.astype(jnp.bfloat16), "enc", 0)
        .astype(jnp.bfloat16)
        .reshape(requests, NL, enc_width)
    )
    cond_mine = cond_gradient(raw_mine, cond_req, enc_gain, encoded_grad)
    slot_grads = collect(cond_mine, "enc", 0)
    cond_delta = jnp.sum(slot_grads.reshape(span_count, NBR, enc_width), axis=1).astype(
        jnp.bfloat16
    )
    delta_cols = lax.dynamic_slice_in_dim(cond_delta, member * enc_cols, enc_cols, 1)
    key_term = contract_first(flat_enc, key_act_grad)
    value_term = contract_first(flat_enc, value_act_grad)
    cond_term = contract_first(summary, delta_cols)
    key_grad, value_grad, cond_grad = tuple(
        (
            part.astype(jnp.float32)
            for part in one_scatter(
                (
                    key_term.astype(jnp.bfloat16),
                    value_term.astype(jnp.bfloat16),
                    cond_term.astype(jnp.bfloat16),
                ),
                "dp",
                (0, 0, 0),
            )
        )
    )
    summary_term = contract_last(delta_cols, w_cond_all)
    normed_term = contract_last(query_act_grad, w_query_all)
    normed_grad, summary_grad = (
        lax.psum(normed_term.astype(jnp.bfloat16), "enc").astype(jnp.float32),
        lax.psum(summary_term.astype(jnp.bfloat16), "enc").astype(jnp.float32),
    )
    scaled = normed_grad * norm_gain
    row_mean = jnp.mean(inputs * scaled, axis=-1, keepdims=True)
    full_grad = (
        grad_rows.astype(jnp.float32)
        + (row_rstd * scaled - inputs * row_rstd**3 * row_mean)
        + jnp.repeat(summary_grad / SPAN, SPAN, axis=0)
    )
    hidden_grad = lax.dynamic_slice_in_dim(full_grad, member * feature_cols, feature_cols, 1)
    return (layer_out, hidden_grad, query_grad, key_grad, value_grad, out_weight_grad, cond_grad)


def solution(mesh):
    placed = (
        P("dp", "enc"),
        P(),
        P("dp", "enc"),
        P("dp", "enc"),
        P("dp", "enc"),
        P("enc", "dp"),
        P("dp", "enc"),
        P(),
        P(("dp", "enc"), None, None),
        P(("dp", "enc")),
        P("dp", "enc"),
    )
    return jax.shard_map(
        shards,
        mesh=mesh,
        in_specs=placed,
        out_specs=(
            P("dp", "enc"),
            P("dp", "enc"),
            P("dp", "enc"),
            P("dp", "enc"),
            P("dp", "enc"),
            P("enc", "dp"),
            P("dp", "enc"),
        ),
        check_vma=False,
    )
```

profile of v0, /device:TPU:0, one launch (start us, length us, event | category | flops | bytes accessed | tf_op | source)
XLA Modules:
  0.0 741.9 jit_solution(10964547584921568469)
XLA Ops:
  11.8 9.6 %all_to_all.40 = s32[4,1,2]{2,1,0:T(1,128)S(1)} all-to-all(s32[4,1,2]{2,1,0:T(1,128)S(1)} %bitcast.99), channel_id=1, replica_groups=mesh['dp'=32,'enc'=4] {'enc'}, dimensions={0} | all-to-all | bytes 64 | tf_op jit(solution)/shard_map/all_to_all | solution.py:157
  30.6 49.5 %all-gather.9.cloned.1.call-done = bf16[512,4096]{1,0:T(8,128)(2,1)} async-done(((bf16[512,1024]{1,0:T(8,128)(2,1)}), bf16[512,4096]{1,0:T(8,128)(2,1)}) %all-gather.9.cloned.1.call-update) | async-done | bytes 4194320 | tf_op jit(solution)/shard_map/all_gather | solution.py:124
  83.1 43.9 %all-gather.11.cloned.1.call-done = bf16[4096,224]{0,1:T(8,128)(2,1)} async-done(((bf16[128,224]{0,1:T(8,128)(2,1)}), bf16[4096,224]{0,1:T(8,128)(2,1)}) %all-gather.11.cloned.1.call-update) | async-done | bytes 1835024 | tf_op jit(solution)/shard_map/all_gather | solution.py:131
  144.0 29.2 %all-gather.21.cloned.1.call-done = bf16[32,28,1024]{2,1,0:T(8,128)(2,1)} async-done(((bf16[1,28,1024]{2,1,0:T(8,128)(2,1)}), bf16[32,28,1024]{2,1,0:T(8,128)(2,1)}) %all-gather.21.cloned.1.call-update) | async-done | bytes 1835024 | tf_op jit(solution)/shard_map/all_gather | solution.py:19
  180.6 40.4 %all-gather.15.cloned.1.call-done = bf16[4096,512]{1,0:T(8,128)(2,1)} async-done(((bf16[128,512]{1,0:T(8,128)(2,1)}), bf16[4096,512]{1,0:T(8,128)(2,1)}) %all-gather.15.cloned.1.call-update) | async-done | bytes 4194320 | tf_op jit(solution)/shard_map/all_gather | solution.py:129
  221.0 5.8 convolution_convert_fusion.11
  227.0 39.4 %all-gather.13.cloned.1.call-done = bf16[16,128,896]{2,1,0:T(8,128)(2,1)} async-done(((bf16[4,128,896]{2,1,0:T(8,128)(2,1)}), bf16[16,128,896]{2,1,0:T(8,128)(2,1)}) %all-gather.13.cloned.1.call-update) | async-done | bytes 3670032 | tf_op jit(solution)/shard_map/all_gather | solution.py:167
  266.4 5.9 convolution_convert_fusion.6
  276.3 6.4 convolution_convert_fusion.7
  291.4 6.0 fusion.34
  297.7 18.7 %all-gather.19.cloned.1.call-done = bf16[512,4096]{1,0:T(8,128)(2,1)} async-done(((bf16[512,1024]{1,0:T(8,128)(2,1)}), bf16[512,4096]{1,0:T(8,128)(2,1)}) %all-gather.19.cloned.1.call-update) | async-done | bytes 4194320 | tf_op jit(solution)/shard_map/all_gather | solution.py:192
  316.4 6.5 convolution_convert_fusion
  323.0 6.5 copy.112
  329.9 38.4 %all-gather.17.cloned.1.call-done = bf16[512,4096]{1,0:T(8,128)(2,1)} async-done(((bf16[512,128]{1,0:T(8,128)(2,1)}), bf16[512,4096]{1,0:T(8,128)(2,1)}) %all-gather.17.cloned.1.call-update) | async-done | bytes 4194320 | tf_op jit(solution)/shard_map/all_gather | solution.py:134
  368.4 5.8 convolution_convert_fusion.10
  378.1 16.3 %fusion.37 = bf16[8,64,4,128]{3,1,2,0:T(8,128)(2,1)} fusion(bf16[8,256,4,128]{3,2,1,0:T(4,128)(2,1)} %reshape.289, f32[8,4,64,256]{3,2,1,0:T(8,128)} %fusion.9, f32[8,4,64,256]{3,2,1,0:T(8,128)} %get-tuple-element.50, f32[8,4,64]{2,1,0:T(4,128)S(1)} %get-tuple-element.49), kind=kOutput, calls=%fused_computation.62 | convolution fusion | flops 138152192 | bytes 6823936 | tf_op jit(solution)/shard_map/chqk,ckhd->cqhd/dot_general | solution.py:210
  395.9 6.8 convolution_convert_fusion.1
  402.7 16.7 %convert_bitcast_fusion.1 = bf16[8,256,4,128]{1,3,2,0:T(8,128)(2,1)} fusion(f32[8,4,64,256]{3,2,1,0:T(8,128)} %fusion.9, bf16[8,64,4,128]{3,2,1,0:T(4,128)(2,1)S(1)} %reshape.288, f32[8,4,64,256]{3,2,1,0:T(8,128)} %get-tuple-element.50, f32[8,4,64]{2,1,0:T(4,128)S(1)} %get-tuple-element.49), kind=kOutput, calls=%fused_computation.29 | convolution fusion | flops 138938624 | bytes 6823936 | tf_op jit(solution)/shard_map/chqk,cqhd->ckhd/dot_general | solution.py:215
  424.4 7.0 convert_bitcast_fusion
  439.5 4.4 add_convert_fusion
  443.9 5.0 all-to-all-start.4
  448.9 6.7 convolution_convert_fusion.2
  461.8 31.0 %all-to-all-done.4 = bf16[4,512,896]{2,1,0:T(8,128)(2,1)} async-done(((bf16[4,512,896]{2,1,0:T(8,128)(2,1)}), bf16[4,512,896]{2,1,0:T(8,128)(2,1)}, u32[]{:S(2)}, u32[]{:S(2)}) %all-to-all-start.4) | async-done | bytes 3670048 | tf_op jit(solution)/shard_map/all_to_all | solution.py:45
  501.4 4.8 convolution_convert_fusion.3
  511.8 4.9 all-to-all-start.3
  520.1 5.0 reshape_reshape.15
  531.0 5.2 reshape.298
  536.3 6.5 convert_element_type.163
  542.8 36.6 %all-to-all-done.3 = bf16[4,512,1024]{2,1,0:T(8,128)(2,1)} async-done(((bf16[4,512,1024]{2,1,0:T(8,128)(2,1)}), bf16[4,512,1024]{2,1,0:T(8,128)(2,1)}, u32[]{:S(2)}, u32[]{:S(2)}) %all-to-all-start.3) | async-done | bytes 4194336 | tf_op jit(solution)/shard_map/all_to_all | solution.py:45
  587.7 58.2 %all-reduce.3.cloned.1.call-done = (bf16[8,4096]{1,0:T(8,128)(2,1)}, bf16[512,4096]{1,0:T(8,128)(2,1)}) async-done(((bf16[8,4096]{1,0:T(8,128)(2,1)}, bf16[512,4096]{1,0:T(8,128)(2,1)}), (bf16[8,4096]{1,0:T(8,128)(2,1)}, bf16[512,4096]{1,0:T(8,128)(2,1)})) %all-reduce.3.cloned.1.call-update) | async-done | bytes 4259856 | tf_op jit(solution)/shard_map/psum | solution.py:263
  645.9 4.9 multiply_reduce_fusion
  655.9 75.2 %reduce-scatter.8.cloned.1.call-done = bf16[448,128]{1,0:T(8,128)(2,1)} async-done(((bf16[14336,128]{1,0:T(8,128)(2,1)}), bf16[448,128]{1,0:T(8,128)(2,1)}) %reduce-scatter.8.cloned.1.call-update) | async-done | bytes 114704 | tf_op jit(solution)/shard_map/reduce_scatter | solution.py:55
  (161 shorter events, 119.5 us)
Async XLA Ops:
  7.2 14.6 %copy-start = (bf16[8,128,896]{2,1,0:T(8,128)(2,1)S(1)}, bf16[8,128,896]{2,1,0:T(8,128)(2,1)}, u32[]{:S(2)}) copy-start(bf16[8,128,896]{2,1,0:T(8,128)(2,1)} %param.19) | copy-start | bytes 5505028
  7.2 72.9 %all-gather.9.cloned.1.call-start = ((), (), s32[]{:S(2)}) async-start(), calls=%async_computation.9 | async-start | bytes 5242880 | tf_op jit(solution)/shard_map/all_gather | solution.py:124
  7.9 119.2 %all-gather.11.cloned.1.call-start = ((), (), s32[]{:S(2)}) async-start(), calls=%async_computation.10 | async-start | bytes 1892352 | tf_op jit(solution)/shard_map/all_gather | solution.py:131
  8.7 164.6 %all-gather.21.cloned.1.call-start = ((), (), s32[]{:S(2)}) async-start(), calls=%async_computation.17 | async-start | bytes 2162688 | tf_op jit(solution)/shard_map/all_gather | solution.py:19
  10.2 210.9 %all-gather.15.cloned.1.call-start = ((), (), s32[]{:S(2)}) async-start(), calls=%async_computation.12 | async-start | bytes 4325376 | tf_op jit(solution)/shard_map/all_gather | solution.py:129
  11.6 129.7 %copy-start.19 = (pred[4]{0:T(512)(128)(4,1)}, pred[4]{0:T(512)(128)(4,1)S(1)}, u32[]{:S(2)}) copy-start(pred[4]{0:T(512)(128)(4,1)S(1)} %get-tuple-element.37) | copy-start | bytes 16
  26.9 102.2 %all-to-all-start.1 = ((bf16[4,2,128,896]{3,2,1,0:T(8,128)(2,1)}), bf16[4,2,128,896]{3,2,1,0:T(8,128)(2,1)S(1)}, u32[]{:S(2)}, u32[]{:S(2)}) async-start(bf16[4,2,128,896]{3,2,1,0:T(8,128)(2,1)} %broadcast_select_fusion), calls=%async_computation.1 | async-start | bytes 3670016 | tf_op jit(solution)/shard_map/all_to_all | solution.py:154
  83.1 58.1 %copy-start.13 = (f32[896]{0:T(1024)S(1)}, f32[896]{0:T(1024)}, u32[]{:S(2)}) copy-start(f32[896]{0:T(1024)} %param.18) | copy-start | bytes 10756
  129.2 5.0 copy-start.4
  129.8 9.7 %all-to-all-start.2 = ((bf16[4,8,224]{2,1,0:T(8,128)(2,1)}), bf16[4,8,224]{2,1,0:T(8,128)(2,1)S(1)}, u32[]{:S(2)}, u32[]{:S(2)}) async-start(bf16[4,8,224]{2,1,0:T(8,128)(2,1)} %broadcast_in_dim.82), calls=%async_computation.2 | async-start | bytes 32768 | tf_op jit(solution)/shard_map/all_to_all | solution.py:30
  134.1 132.3 %all-gather.13.cloned.1.call-start = ((), (), s32[]{:S(2)}) async-start(), calls=%async_computation.11 | async-start | bytes 4587520 | tf_op jit(solution)/shard_map/all_gather | solution.py:167
  141.3 35.7 %copy-start.15 = (f32[4,128]{1,0:T(4,128)}, f32[4,128]{1,0:T(4,128)S(1)}, u32[]{:S(2)}) copy-start(f32[4,128]{1,0:T(4,128)S(1)} %get-tuple-element.46) | copy-start | bytes 6148
  142.6 173.8 %all-gather.19.cloned.1.call-start = ((), (), s32[]{:S(2)}) async-start(), calls=%async_computation.14 | async-start | bytes 5242880 | tf_op jit(solution)/shard_map/all_gather | solution.py:192
  143.2 225.1 %all-gather.17.cloned.1.call-start = ((), (), s32[]{:S(2)}) async-start(), calls=%async_computation.13 | async-start | bytes 4325376 | tf_op jit(solution)/shard_map/all_gather | solution.py:134
  144.0 440.3 %reduce-scatter.10.cloned.1.call-start = ((), (), s32[]{:S(2)}) async-start(), calls=%async_computation.18 | async-start | bytes 4325376
  177.0 44.1 %copy-start.17 = (f32[4096]{0:T(1024)S(1)}, f32[4096]{0:T(1024)}, u32[]{:S(2)}) copy-start(f32[4096]{0:T(1024)} %param.12) | copy-start | bytes 49156
  180.6 215.2 %copy-start.22 = (f32[512]{0:T(512)}, f32[512]{0:T(512)S(1)}, u32[]{:S(2)}) copy-start(f32[512]{0:T(512)S(1)} %get-tuple-element.44) | copy-start | bytes 6148
  329.5 256.6 %reduce-scatter.6.cloned.1.call-start = ((), (), s32[]{:S(2)}) async-start(), calls=%async_computation.15 | async-start | bytes 4325376 | tf_op jit(solution)/shard_map/reduce_scatter | solution.py:224
  443.9 48.9 %all-to-all-start.4 = ((bf16[4,512,896]{2,1,0:T(8,128)(2,1)}), bf16[4,512,896]{2,1,0:T(8,128)(2,1)}, u32[]{:S(2)}, u32[]{:S(2)}) async-start(bf16[4,512,896]{2,1,0:T(8,128)(2,1)} %bitcast.88), calls=%async_computation.4 | async-start | bytes 7340032 | tf_op jit(solution)/shard_map/all_to_all | solution.py:45
  448.9 6.7 copy-start.8
  448.9 6.7 copy-start.25
  461.7 34.2 %copy-start.14 = (f32[896]{0:T(1024)S(1)}, f32[896]{0:T(1024)}, u32[]{:S(2)}) copy-start(f32[896]{0:T(1024)} %param.18) | copy-start | bytes 10756
  461.7 34.2 %copy-start.20 = (pred[4]{0:T(512)(128)(4,1)S(1)}, pred[4]{0:T(512)(128)(4,1)}, u32[]{:S(2)}) copy-start(pred[4]{0:T(512)(128)(4,1)} %copy-done.19) | copy-start | bytes 16
  461.7 34.7 %copy-start.16 = (f32[4,128]{1,0:T(4,128)S(1)}, f32[4,128]{1,0:T(4,128)}, u32[]{:S(2)}) copy-start(f32[4,128]{1,0:T(4,128)} %copy-done.15) | copy-start | bytes 6148
  461.8 34.7 %copy-start.24 = (f32[4,128]{1,0:T(4,128)S(1)}, f32[4,128]{1,0:T(4,128)}, u32[]{:S(2)}) copy-start(f32[4,128]{1,0:T(4,128)} %get-tuple-element.45) | copy-start | bytes 6148
  497.9 13.9 %all-to-all-start.5 = ((f32[4,4,896]{2,1,0:T(4,128)}), f32[4,4,896]{2,1,0:T(4,128)S(1)}, u32[]{:S(2)}, u32[]{:S(2)}) async-start(f32[4,4,896]{2,1,0:T(4,128)} %broadcast_in_dim.84), calls=%async_computation.5 | async-start | bytes 114688 | tf_op jit(solution)/shard_map/all_to_all | solution.py:30
  511.8 67.6 %all-to-all-start.3 = ((bf16[4,512,1024]{2,1,0:T(8,128)(2,1)}), bf16[4,512,1024]{2,1,0:T(8,128)(2,1)}, u32[]{:S(2)}, u32[]{:S(2)}) async-start(bf16[4,512,1024]{2,1,0:T(8,128)(2,1)} %bitcast.80), calls=%async_computation.3 | async-start | bytes 8388608 | tf_op jit(solution)/shard_map/all_to_all | solution.py:45
  516.7 129.2 %all-reduce.3.cloned.1.call-start = ((), (), s32[]{:S(2)}) async-start(), calls=%async_computation.19 | async-start | bytes 8519680 | tf_op jit(solution)/shard_map/psum | solution.py:263
  527.7 203.4 %reduce-scatter.8.cloned.1.call-start = ((), (), s32[]{:S(2)}) async-start(), calls=%async_computation.16 | async-start | bytes 3784704 | tf_op jit(solution)/shard_map/reduce_scatter | solution.py:55
  542.8 40.1 %copy-start.3 = (bf16[512,1024]{1,0:T(8,128)(2,1)S(1)}, bf16[512,1024]{1,0:T(8,128)(2,1)}, u32[]{:S(2)}) copy-start(bf16[512,1024]{1,0:T(8,128)(2,1)} %param.11) | copy-start | bytes 3145732
  582.9 63.0 %copy-start.18 = (f32[4096]{0:T(1024)S(1)}, f32[4096]{0:T(1024)}, u32[]{:S(2)}) copy-start(f32[4096]{0:T(1024)} %param.12) | copy-start | bytes 49156
  651.9 83.0 %copy-start.1 = (bf16[8,128,896]{2,1,0:T(8,128)(2,1)S(1)}, bf16[8,128,896]{2,1,0:T(8,128)(2,1)}, u32[]{:S(2)}) copy-start(bf16[8,128,896]{2,1,0:T(8,128)(2,1)} %param.19) | copy-start | bytes 5505028
  (10 other events, 24.7 us)
Sparse Core Ops, SparseCore 0:
  9.7 70.3 all-gather.8
  82.3 44.7 all-gather.10
  129.9 43.2 all-gather.20
  175.4 45.6 all-gather.14
  223.1 43.2 all-gather.12
  267.9 48.4 all-gather.18
  318.6 49.7 all-gather.16
  372.0 81.5 reduce-scatter.9
  457.7 81.2 reduce-scatter.5
  541.9 103.9 all-reduce.2
  650.0 81.0 reduce-scatter.7
where the time goes:
time: 752 us; the launch traced here: 742 us
  waiting for transfers between devices  467 us (62%)
  matrix products  119 us (16%)
  local copies, waits for them, and re-layouts  60.3 us (8%)
  other arithmetic  48.4 us (6%)
  starting transfers between devices  22.4 us (3%)
  between operations  14.9 us (2%)
  blocking collectives  9.59 us (1%)
    reduce_scatter x1, waiting for transfers between devices, one_scatter(): lax.psum_scatter(lines, axis, tiled=True).reshape(-1)  75.2 us
    all_to_all x2, waiting for transfers between devices, summed_on_arrival(): tiles = lax.all_to_all(in_blocks(shard, dim, peers), axis, 0, 0, tiled=True)  67.6 us
    psum x1, waiting for transfers between devices, shards(): lax.psum(summary_term.astype(jnp.bfloat16), 'enc').astype(jnp.float32)  58.2 us
    all_gather x1, waiting for transfers between devices, shards(): full_rows = lax.all_gather(hidden, 'enc', axis=1, tiled=True)  49.5 us
    all_gather x1, waiting for transfers between devices, shards(): lax.all_gather(w_cond, 'dp', axis=0, tiled=True)  43.9 us
    all_gather x1, waiting for transfers between devices, shards(): lax.all_gather(w_query, 'dp', axis=0, tiled=True)  40.4 us
    all_gather x1, waiting for transfers between devices, shards(): encoded = lax.all_gather(encoded_mine, 'enc', axis=0, tiled=True)  39.4 us
    all_gather x1, waiting for transfers between devices, shards(): w_out_all = lax.all_gather(w_out, 'dp', axis=1, tiled=True)  38.4 us
  transfers between devices with their start and end apart: 16, of which 12 were waited for; matrix products, arithmetic and copies ran while one was open for 30% of the time, Pallas kernels for 0%

commit v1 on v0

--- a/solution.py
+++ b/solution.py
@@ -121,7 +121,12 @@
     heads_here = head_cols // HSZ
     keys_len = NBR * NL
     score_scale = HSZ ** (-0.5)
-    full_rows = lax.all_gather(hidden, "enc", axis=1, tiled=True)
+    ring = [hidden]
+    for hop in range(3):
+        ring.append(lax.ppermute(ring[-1], "enc", [(dev, (dev + 1) % 4) for dev in range(4)]))
+    full_rows = jnp.roll(
+        jnp.concatenate(ring[::-1], axis=1), (lax.axis_index("enc") + 1) * ring[0].shape[1], axis=1
+    )
     inputs = full_rows.astype(jnp.float32)
     row_rstd = rms_scale(inputs)
     normed = (inputs * row_rstd * norm_gain).astype(jnp.bfloat16)

time: 752 us -> 685 us (0.911)
  waiting for transfers between devices: 467 us -> 390 us
  local copies, waits for them, and re-layouts: 60.3 us -> 75.3 us
  blocking collectives: 9.59 us -> 0 us
    ppermute x0 -> x3, waiting for transfers between devices: none -> 61.9 us  [shards(): lax.ppermute(ring[-1], 'enc', [(dev, (dev + 1) % 4) for dev in range(4)])]
    all_gather x1 -> x0, waiting for transfers between devices: 49.5 us -> none  [shards(): full_rows = lax.all_gather(hidden, 'enc', axis=1, tiled=True)]
    all_gather x1, waiting for transfers between devices: 43.9 us -> 0.02 us  [shards(): lax.all_gather(w_cond, 'dp', axis=0, tiled=True)]
    all_gather x1, waiting for transfers between devices: 29.2 us -> 0.01 us  [side_by_side(): lax.all_gather(both, axis, axis=dim, tiled=True)]
    all_gather x1, waiting for transfers between devices: 40.4 us -> 23.4 us  [shards(): lax.all_gather(w_query, 'dp', axis=0, tiled=True)]
    unnamed x58 -> x67, local copies, waits for them, and re-layouts: 17.1 us -> 26.7 us
    all_to_all x1 -> x0, blocking collectives: 9.59 us -> none  [shards(): lax.all_to_all(row_buffer, 'enc', split_axis=0, concat_axis=0, tiled=True)]
  transfers between devices with their start and end apart: 16 -> 19, of which waited for: 12 -> 13; matrix products, arithmetic and copies ran while one was open for 30% -> 34% of each run, Pallas kernels for 0% -> 0%
where the time goes in v1:
time: 685 us; the launch traced here: 679 us
  waiting for transfers between devices  390 us (57%)
  matrix products  121 us (18%)
  local copies, waits for them, and re-layouts  75.3 us (11%)
  other arithmetic  47.9 us (7%)
  starting transfers between devices  29.4 us (4%)
  between operations  15.2 us (2%)
    reduce_scatter x1, waiting for transfers between devices, one_scatter(): lax.psum_scatter(lines, axis, tiled=True).reshape(-1)  75.1 us
    all_to_all x2, waiting for transfers between devices, summed_on_arrival(): tiles = lax.all_to_all(in_blocks(shard, dim, peers), axis, 0, 0, tiled=True)  72.8 us
    ppermute x3, waiting for transfers between devices, shards(): lax.ppermute(ring[-1], 'enc', [(dev, (dev + 1) % 4) for dev in range(4)])  61.9 us
    psum x1, waiting for transfers between devices, shards(): lax.psum(summary_term.astype(jnp.bfloat16), 'enc').astype(jnp.float32)  52.2 us
    all_gather x1, waiting for transfers between devices, shards(): encoded = lax.all_gather(encoded_mine, 'enc', axis=0, tiled=True)  39.4 us
    all_gather x1, waiting for transfers between devices, shards(): w_out_all = lax.all_gather(w_out, 'dp', axis=1, tiled=True)  38.2 us
    unnamed x67, local copies, waits for them, and re-layouts  26.7 us
    all_gather x1, waiting for transfers between devices, shards(): lax.all_gather(w_query, 'dp', axis=0, tiled=True)  23.4 us
  transfers between devices with their start and end apart: 19, of which 13 were waited for; matrix products, arithmetic and copies ran while one was open for 34% of the time, Pallas kernels for 0%

profile of v1, /device:TPU:0, one launch (start us, length us, event | category | flops | bytes accessed | tf_op | source)
XLA Modules:
  0.0 678.6 jit_solution(17137030095943042444)
XLA Ops:
  11.9 24.8 %collective-permute-done = bf16[512,1024]{1,0:T(8,128)(2,1)S(1)} collective-permute-done((bf16[512,1024]{1,0:T(8,128)(2,1)}, bf16[512,1024]{1,0:T(8,128)(2,1)S(1)}, u32[]{:S(2)}, u32[]{:S(2)}) %collective-permute-start) | collective-permute-done | bytes 1048608 | tf_op jit(solution)/shard_map/ppermute | solution.py:126
  42.8 19.4 %collective-permute-done.1 = bf16[512,1024]{1,0:T(8,128)(2,1)} collective-permute-done((bf16[512,1024]{1,0:T(8,128)(2,1)S(1)}, bf16[512,1024]{1,0:T(8,128)(2,1)}, u32[]{:S(2)}, u32[]{:S(2)}) %collective-permute-start.1) | collective-permute-done | bytes 1048608 | tf_op jit(solution)/shard_map/ppermute | solution.py:126
  67.6 4.5 all-to-all-start.1
  72.1 17.7 %collective-permute-done.2 = bf16[512,1024]{1,0:T(8,128)(2,1)} collective-permute-done((bf16[512,1024]{1,0:T(8,128)(2,1)}, bf16[512,1024]{1,0:T(8,128)(2,1)}, u32[]{:S(2)}, u32[]{:S(2)}) %collective-permute-start.2) | collective-permute-done | bytes 1048608 | tf_op jit(solution)/shard_map/ppermute | solution.py:126
  101.9 4.7 all-to-all-done.1
  127.8 23.4 %all-gather.12.cloned.1.call-done = bf16[4096,512]{1,0:T(8,128)(2,1)} async-done(((bf16[128,512]{1,0:T(8,128)(2,1)}), bf16[4096,512]{1,0:T(8,128)(2,1)}) %all-gather.12.cloned.1.call-update) | async-done | bytes 4194320 | tf_op jit(solution)/shard_map/all_gather | solution.py:134
  151.2 5.8 convolution_convert_fusion.11
  157.2 39.4 %all-gather.10.cloned.1.call-done = bf16[16,128,896]{2,1,0:T(8,128)(2,1)} async-done(((bf16[4,128,896]{2,1,0:T(8,128)(2,1)}), bf16[16,128,896]{2,1,0:T(8,128)(2,1)}) %all-gather.10.cloned.1.call-update) | async-done | bytes 3670032 | tf_op jit(solution)/shard_map/all_gather | solution.py:172
  196.6 5.9 convolution_convert_fusion.6
  206.5 6.4 convolution_convert_fusion.7
  221.6 6.8 fusion.34
  229.8 16.8 %all-gather.16.cloned.1.call-done = bf16[512,4096]{1,0:T(8,128)(2,1)} async-done(((bf16[512,1024]{1,0:T(8,128)(2,1)}), bf16[512,4096]{1,0:T(8,128)(2,1)}) %all-gather.16.cloned.1.call-update) | async-done | bytes 4194320 | tf_op jit(solution)/shard_map/all_gather | solution.py:197
  246.6 6.5 convolution_convert_fusion
  253.1 6.5 copy.112
  260.2 38.2 %all-gather.14.cloned.1.call-done = bf16[512,4096]{1,0:T(8,128)(2,1)} async-done(((bf16[512,128]{1,0:T(8,128)(2,1)}), bf16[512,4096]{1,0:T(8,128)(2,1)}) %all-gather.14.cloned.1.call-update) | async-done | bytes 4194320 | tf_op jit(solution)/shard_map/all_gather | solution.py:139
  298.4 6.6 convolution_convert_fusion.10
  310.9 16.3 %fusion.37 = bf16[8,64,4,128]{3,1,2,0:T(8,128)(2,1)} fusion(bf16[8,256,4,128]{3,2,1,0:T(4,128)(2,1)} %reshape.289, f32[8,4,64,256]{3,2,1,0:T(8,128)} %fusion.9, f32[8,4,64,256]{3,2,1,0:T(8,128)} %get-tuple-element.50, f32[8,4,64]{2,1,0:T(4,128)S(1)} %get-tuple-element.49), kind=kOutput, calls=%fused_computation.63 | convolution fusion | flops 138152192 | bytes 6823936 | tf_op jit(solution)/shard_map/chqk,ckhd->cqhd/dot_general | solution.py:215
  329.5 6.8 %convolution_convert_fusion.1 = bf16[4096,512]{1,0:T(8,128)(2,1)} fusion(f32[4096]{0:T(1024)S(1)} %copy-done.20, f32[512]{0:T(512)S(1)} %get-tuple-element.44, bf16[512,8192]{1,0:T(8,128)(2,1)} %copy-done.2, s32[]{:T(128)S(6)} %select_n.119, bf16[64,8,4,128]{3,2,1,0:T(4,128)(2,1)S(1)} %bitcast.94), kind=kOutput, calls=%fused_computation.13 | convolution fusion | flops 2157969408 | bytes 8931332 | tf_op jit(solution)/shard_map/dot_general | solution.py:85
  336.4 16.5 %convert_bitcast_fusion.1 = bf16[8,256,4,128]{1,3,2,0:T(8,128)(2,1)} fusion(f32[8,4,64,256]{3,2,1,0:T(8,128)} %fusion.9, bf16[8,64,4,128]{3,2,1,0:T(4,128)(2,1)S(1)} %reshape.288, f32[8,4,64,256]{3,2,1,0:T(8,128)} %get-tuple-element.50, f32[8,4,64]{2,1,0:T(4,128)S(1)} %get-tuple-element.49), kind=kOutput, calls=%fused_computation.30 | convolution fusion | flops 138938624 | bytes 6823936 | tf_op jit(solution)/shard_map/chqk,cqhd->ckhd/dot_general | solution.py:220
  357.9 7.0 %convert_bitcast_fusion = bf16[8,256,4,128]{1,3,2,0:T(8,128)(2,1)} fusion(bf16[8,64,4,128]{3,2,1,0:T(4,128)(2,1)S(1)} %copy-done.7, f32[8,4,64]{2,1,0:T(4,128)S(1)} %get-tuple-element.49, f32[8,4,64,256]{3,2,1,0:T(8,128)} %copy-done.4), kind=kOutput, calls=%fused_computation.29 | convolution fusion | flops 137365760 | bytes 4726784 | tf_op jit(solution)/shard_map/chqk,cqhd->ckhd/dot_general | solution.py:225
  377.4 5.1 all-to-all-start.4
  382.5 6.7 convolution_convert_fusion.2
  395.3 31.1 %all-to-all-done.4 = bf16[4,512,896]{2,1,0:T(8,128)(2,1)} async-done(((bf16[4,512,896]{2,1,0:T(8,128)(2,1)}), bf16[4,512,896]{2,1,0:T(8,128)(2,1)}, u32[]{:S(2)}, u32[]{:S(2)}) %all-to-all-start.4) | async-done | bytes 3670048 | tf_op jit(solution)/shard_map/all_to_all | solution.py:45
  437.0 4.6 convolution_convert_fusion.3
  448.0 4.8 all-to-all-start.3
  457.1 5.0 reshape_reshape.15
  468.1 5.3 reshape.298
  473.5 6.8 %dynamic-slice_convert_fusion = f32[512,4096]{1,0:T(8,128)} fusion(bf16[512,8192]{1,0:T(8,128)(2,1)} %copy-done.2, s32[]{:T(128)S(6)} %select_n.119), kind=kLoop, calls=%fused_computation.22 | loop fusion | flops 2097152 | bytes 12582916 | tf_op jit(solution)/shard_map/convert_element_type | solution.py:130
  480.3 41.6 %all-to-all-done.3 = bf16[4,512,1024]{2,1,0:T(8,128)(2,1)} async-done(((bf16[4,512,1024]{2,1,0:T(8,128)(2,1)}), bf16[4,512,1024]{2,1,0:T(8,128)(2,1)}, u32[]{:S(2)}, u32[]{:S(2)}) %all-to-all-start.3) | async-done | bytes 4194336 | tf_op jit(solution)/shard_map/all_to_all | solution.py:45
  530.2 52.2 %all-reduce.3.cloned.1.call-done = (bf16[8,4096]{1,0:T(8,128)(2,1)}, bf16[512,4096]{1,0:T(8,128)(2,1)}) async-done(((bf16[8,4096]{1,0:T(8,128)(2,1)}, bf16[512,4096]{1,0:T(8,128)(2,1)}), (bf16[8,4096]{1,0:T(8,128)(2,1)}, bf16[512,4096]{1,0:T(8,128)(2,1)})) %all-reduce.3.cloned.1.call-update) | async-done | bytes 4259856 | tf_op jit(solution)/shard_map/psum | solution.py:268
  582.4 4.9 multiply_reduce_fusion
  592.4 75.1 %reduce-scatter.8.cloned.1.call-done = bf16[448,128]{1,0:T(8,128)(2,1)} async-done(((bf16[14336,128]{1,0:T(8,128)(2,1)}), bf16[448,128]{1,0:T(8,128)(2,1)}) %reduce-scatter.8.cloned.1.call-update) | async-done | bytes 114704 | tf_op jit(solution)/shard_map/reduce_scatter | solution.py:55
  (174 shorter events, 139.8 us)
Async XLA Ops:
  7.2 55.5 %copy-start = (bf16[8,128,896]{2,1,0:T(8,128)(2,1)S(1)}, bf16[8,128,896]{2,1,0:T(8,128)(2,1)}, u32[]{:S(2)}) copy-start(bf16[8,128,896]{2,1,0:T(8,128)(2,1)} %param.19) | copy-start | bytes 5505028
  7.2 92.7 %all-gather.8.cloned.1.call-start = ((), (), s32[]{:S(2)}) async-start(), calls=%async_computation.9 | async-start | bytes 1892352 | tf_op jit(solution)/shard_map/all_gather | solution.py:136
  7.9 116.2 %all-gather.18.cloned.1.call-start = ((), (), s32[]{:S(2)}) async-start(), calls=%async_computation.16 | async-start | bytes 2162688 | tf_op jit(solution)/shard_map/all_gather | solution.py:19
  9.4 141.8 %all-gather.12.cloned.1.call-start = ((), (), s32[]{:S(2)}) async-start(), calls=%async_computation.11 | async-start | bytes 4325376 | tf_op jit(solution)/shard_map/all_gather | solution.py:134
  10.1 26.5 %collective-permute-start = (bf16[512,1024]{1,0:T(8,128)(2,1)}, bf16[512,1024]{1,0:T(8,128)(2,1)S(1)}, u32[]{:S(2)}, u32[]{:S(2)}) collective-permute-start(bf16[512,1024]{1,0:T(8,128)(2,1)} %param.11), channel_id=1, source_target_pairs={{0,1},{1,2},{2,3},{3,0},{4,5},{5,6},{6,7},{7,4},{8,9},{9,10},{10,1... | collective-permute-start | bytes 3145736 | tf_op jit(solution)/shard_map/ppermute | solution.py:126
  36.7 31.0 %copy-start.5 = (bf16[512,1024]{1,0:T(8,128)(2,1)}, bf16[512,1024]{1,0:T(8,128)(2,1)S(1)}, u32[]{:S(2)}) copy-start(bf16[512,1024]{1,0:T(8,128)(2,1)S(1)} %collective-permute-done) | copy-start | bytes 3145732
  36.7 25.5 %collective-permute-start.1 = (bf16[512,1024]{1,0:T(8,128)(2,1)S(1)}, bf16[512,1024]{1,0:T(8,128)(2,1)}, u32[]{:S(2)}, u32[]{:S(2)}) collective-permute-start(bf16[512,1024]{1,0:T(8,128)(2,1)S(1)} %collective-permute-done), channel_id=1, source_target_pairs={{0,1},{1,2},{2,3},{3,0},{4,5},{5,6},{6,7},{7,4},{8,9},{9,10},{10,1... | collective-permute-start | bytes 3145736 | tf_op jit(solution)/shard_map/ppermute | solution.py:126
  37.9 79.8 %copy-start.22 = (pred[4]{0:T(512)(128)(4,1)}, pred[4]{0:T(512)(128)(4,1)S(1)}, u32[]{:S(2)}) copy-start(pred[4]{0:T(512)(128)(4,1)S(1)} %get-tuple-element.37) | copy-start | bytes 16
  38.6 23.6 %all-to-all-start = ((s32[4,1,2]{2,1,0:T(1,128)}), s32[4,1,2]{2,1,0:T(1,128)S(1)}, u32[]{:S(2)}, u32[]{:S(2)}) async-start(s32[4,1,2]{2,1,0:T(1,128)} %bitcast), calls=%async_computation | async-start | bytes 4096 | tf_op jit(solution)/shard_map/all_to_all | solution.py:162
  62.2 27.6 %collective-permute-start.2 = (bf16[512,1024]{1,0:T(8,128)(2,1)}, bf16[512,1024]{1,0:T(8,128)(2,1)}, u32[]{:S(2)}, u32[]{:S(2)}) collective-permute-start(bf16[512,1024]{1,0:T(8,128)(2,1)} %collective-permute-done.1), channel_id=1, source_target_pairs={{0,1},{1,2},{2,3},{3,0},{4,5},{5,6},{6,7},{7,4},{8,9},{9,10},{10,1... | collective-permute-start | bytes 3145736 | tf_op jit(solution)/shard_map/ppermute | solution.py:126
  67.6 39.0 %all-to-all-start.1 = ((bf16[4,2,128,896]{3,2,1,0:T(8,128)(2,1)}), bf16[4,2,128,896]{3,2,1,0:T(8,128)(2,1)}, u32[]{:S(2)}, u32[]{:S(2)}) async-start(bf16[4,2,128,896]{3,2,1,0:T(8,128)(2,1)} %broadcast_select_fusion), calls=%async_computation.1 | async-start | bytes 3670016 | tf_op jit(solution)/shard_map/all_to_all | solution.py:159
  72.1 20.4 %copy-start.6 = (bf16[512,1024]{1,0:T(8,128)(2,1)S(1)}, bf16[512,1024]{1,0:T(8,128)(2,1)}, u32[]{:S(2)}) copy-start(bf16[512,1024]{1,0:T(8,128)(2,1)} %copy-done.5) | copy-start | bytes 3145732
  99.8 17.8 %copy-start.18 = (f32[896]{0:T(1024)S(1)}, f32[896]{0:T(1024)}, u32[]{:S(2)}) copy-start(f32[896]{0:T(1024)} %param.18) | copy-start | bytes 10756
  107.3 8.6 %all-to-all-start.2 = ((bf16[4,8,224]{2,1,0:T(8,128)(2,1)}), bf16[4,8,224]{2,1,0:T(8,128)(2,1)S(1)}, u32[]{:S(2)}, u32[]{:S(2)}) async-start(bf16[4,8,224]{2,1,0:T(8,128)(2,1)} %broadcast_in_dim.82), calls=%async_computation.2 | async-start | bytes 32768 | tf_op jit(solution)/shard_map/all_to_all | solution.py:30
  110.5 86.0 %all-gather.10.cloned.1.call-start = ((), (), s32[]{:S(2)}) async-start(), calls=%async_computation.10 | async-start | bytes 4587520 | tf_op jit(solution)/shard_map/all_gather | solution.py:172
  117.6 5.9 copy-start.19
  119.0 127.6 %all-gather.16.cloned.1.call-start = ((), (), s32[]{:S(2)}) async-start(), calls=%async_computation.13 | async-start | bytes 5242880 | tf_op jit(solution)/shard_map/all_gather | solution.py:197
  119.6 178.8 %all-gather.14.cloned.1.call-start = ((), (), s32[]{:S(2)}) async-start(), calls=%async_computation.12 | async-start | bytes 4325376 | tf_op jit(solution)/shard_map/all_gather | solution.py:139
  120.2 406.6 %reduce-scatter.10.cloned.1.call-start = ((), (), s32[]{:S(2)}) async-start(), calls=%async_computation.17 | async-start | bytes 4325376
  123.5 27.7 %copy-start.20 = (f32[4096]{0:T(1024)S(1)}, f32[4096]{0:T(1024)}, u32[]{:S(2)}) copy-start(f32[4096]{0:T(1024)} %param.12) | copy-start | bytes 49156
  124.1 204.6 %copy-start.24 = (f32[512]{0:T(512)}, f32[512]{0:T(512)S(1)}, u32[]{:S(2)}) copy-start(f32[512]{0:T(512)S(1)} %get-tuple-element.44) | copy-start | bytes 6148
  259.7 268.8 %reduce-scatter.6.cloned.1.call-start = ((), (), s32[]{:S(2)}) async-start(), calls=%async_computation.14 | async-start | bytes 4325376 | tf_op jit(solution)/shard_map/reduce_scatter | solution.py:229
  377.4 5.1 copy-start.16
  377.4 49.1 %all-to-all-start.4 = ((bf16[4,512,896]{2,1,0:T(8,128)(2,1)}), bf16[4,512,896]{2,1,0:T(8,128)(2,1)}, u32[]{:S(2)}, u32[]{:S(2)}) async-start(bf16[4,512,896]{2,1,0:T(8,128)(2,1)} %bitcast.87), calls=%async_computation.4 | async-start | bytes 7340032 | tf_op jit(solution)/shard_map/all_to_all | solution.py:45
  382.5 6.7 copy-start.11
  382.5 6.7 copy-start.26
  432.9 15.2 %all-to-all-start.5 = ((f32[4,4,896]{2,1,0:T(4,128)}), f32[4,4,896]{2,1,0:T(4,128)}, u32[]{:S(2)}, u32[]{:S(2)}) async-start(f32[4,4,896]{2,1,0:T(4,128)} %broadcast_in_dim.84), calls=%async_computation.5 | async-start | bytes 114688 | tf_op jit(solution)/shard_map/all_to_all | solution.py:30
  448.0 73.9 %all-to-all-start.3 = ((bf16[4,512,1024]{2,1,0:T(8,128)(2,1)}), bf16[4,512,1024]{2,1,0:T(8,128)(2,1)}, u32[]{:S(2)}, u32[]{:S(2)}) async-start(bf16[4,512,1024]{2,1,0:T(8,128)(2,1)} %bitcast.80), calls=%async_computation.3 | async-start | bytes 8388608 | tf_op jit(solution)/shard_map/all_to_all | solution.py:45
  452.9 129.5 %all-reduce.3.cloned.1.call-start = ((), (), s32[]{:S(2)}) async-start(), calls=%async_computation.18 | async-start | bytes 8519680 | tf_op jit(solution)/shard_map/psum | solution.py:268
  464.7 202.8 %reduce-scatter.8.cloned.1.call-start = ((), (), s32[]{:S(2)}) async-start(), calls=%async_computation.15 | async-start | bytes 3784704 | tf_op jit(solution)/shard_map/reduce_scatter | solution.py:55
  525.4 57.0 %copy-start.21 = (f32[4096]{0:T(1024)S(1)}, f32[4096]{0:T(1024)}, u32[]{:S(2)}) copy-start(f32[4096]{0:T(1024)} %param.12) | copy-start | bytes 49156
  588.4 82.8 %copy-start.1 = (bf16[8,128,896]{2,1,0:T(8,128)(2,1)S(1)}, bf16[8,128,896]{2,1,0:T(8,128)(2,1)}, u32[]{:S(2)}) copy-start(bf16[8,128,896]{2,1,0:T(8,128)(2,1)} %param.19) | copy-start | bytes 5505028
  (14 other events, 33.2 us)
Sparse Core Ops, SparseCore 0:
  10.2 46.8 all-gather.7
  60.0 43.1 all-gather.17
  105.5 45.7 all-gather.11
  153.3 43.2 all-gather.9
  198.1 48.4 all-gather.15
  248.6 49.7 all-gather.13
  302.0 81.5 reduce-scatter.9
  387.7 81.2 reduce-scatter.5
  472.1 110.3 all-reduce.2
  586.4 81.0 reduce-scatter.7
